TPU v7x, 32 devices: a whole 2x2x4 slice. The times are simulated.
32 devices in a mesh: ray: 4 (over x, core), vox: 8 (over z, y).
Axes of the slice: x: 2, y: 2, z: 4, core: 2. Of those that a mesh axis runs over, the one named last changes fastest.
Arguments:
- tiles: float32 [2048, 128, 128], P(('ray', 'vox')), may hold values from -0.25 to 0.25
- tile_ray: int32 [2048], P(('ray', 'vox')), may hold values from 0 to 15
- tile_vox: int32 [2048], P(('ray', 'vox')), may hold values from 0 to 511, as said below
- tile_count: int32 [32], P(('ray', 'vox')), may hold values from 1 to 64, as said below
- travel: float32 [512, 128], P(('ray', 'vox')), may hold values from -6 to 6
Outputs:
- solution: float32 [512, 128], P('vox')
- direction: float32 [512, 128], P('vox')
Inputs may be any that keep to these rules, and one draw needn't show every extreme that they name: `tile_count`: each entry is 1 to 64; some device has exactly 64 live slots. Among the 64 slots of one device (live or not), at most 16 have voxel blocks in the same range of 64 blocks (same tile_vox // 64); on every device some range is named by exactly 16 slots.
All inputs are finite; a program needn't handle non-finite values.
Results may differ from a plain program's by a relative error of at most 0.00017.
Values sent between devices are 32-bit elements; how exact they have to be, the bound alone decides.
No kernel may reach another device: no remote copies, remote signals or barrier semaphores. Data moves between devices by JAX's collectives and lax.ppermute only.
A program may use at most 64 MiB of HBM per device.

v0:
```python
import jax
import jax.numpy as jnp
from jax import lax
from jax.sharding import PartitionSpec as P

VBD = 64
ITERS = 2
HIGH = lax.Precision.HIGHEST


def on_device(tiles, tile_ray, tile_vox, tile_count, travel):
    n_vox = lax.axis_size("vox")
    blocks_all = VBD * n_vox
    tile_num = tiles.shape[0]
    ray_blocks = travel.shape[0]
    width = travel.shape[1]
    live = (jnp.arange(tile_num, dtype=jnp.int32) < tile_count[0]).astype(jnp.float32)[:, None]
    selector = (tile_ray[None, :] == jnp.arange(ray_blocks, dtype=jnp.int32)[:, None]).astype(
        jnp.float32
    )

    def backward(ray_vec):
        rows_in = jnp.dot(selector.T, ray_vec, precision=HIGH)
        prod = jnp.einsum("tij,ti->tj", tiles, rows_in, precision=HIGH) * live
        partial_sum = jnp.zeros((blocks_all, width), jnp.float32).at[tile_vox].add(prod)
        owned = lax.psum_scatter(partial_sum, "vox", scatter_dimension=0, tiled=True)
        return lax.psum(owned, "ray")

    def ray_length(ray_vec):
        return jnp.sqrt(lax.psum(jnp.sum(ray_vec * ray_vec), ("ray", "vox")))

    def vox_length(vox_vec):
        return jnp.sqrt(lax.psum(jnp.sum(vox_vec * vox_vec), "vox"))

    beta_now = ray_length(travel)
    ray_vec = travel / beta_now
    vox_vec = backward(ray_vec)
    alpha_now = vox_length(vox_vec)
    vox_vec = vox_vec / alpha_now
    direction = vox_vec
    solution = jnp.zeros_like(vox_vec)
    phibar = beta_now
    rhobar = alpha_now
    for step in range(ITERS):
        whole = lax.all_gather(vox_vec, "vox", axis=0, tiled=True)
        forward_prod = jnp.einsum("tij,tj->ti", tiles, whole[tile_vox], precision=HIGH) * live
        ray_vec = jnp.dot(selector, forward_prod, precision=HIGH) - alpha_now * ray_vec
        beta_now = ray_length(ray_vec)
        ray_vec = ray_vec / beta_now
        vox_vec = backward(ray_vec) - beta_now * vox_vec
        alpha_now = vox_length(vox_vec)
        vox_vec = vox_vec / alpha_now
        rho_val = jnp.sqrt(rhobar * rhobar + beta_now * beta_now)
        cosine = rhobar / rho_val
        sine_val = beta_now / rho_val
        theta_val = sine_val * alpha_now
        rhobar = -cosine * alpha_now
        phi_val = cosine * phibar
        phibar = sine_val * phibar
        solution = solution + phi_val / rho_val * direction
        direction = vox_vec - theta_val / rho_val * direction
    return (solution, direction)


def solution(mesh):
    return jax.shard_map(
        on_device,
        mesh=mesh,
        in_specs=(
            P(("ray", "vox"), None, None),
            P(("ray", "vox")),
            P(("ray", "vox")),
            P(("ray", "vox")),
            P(("ray", "vox"), None),
        ),
        out_specs=(P("vox", None), P("vox", None)),
        check_vma=False,
    )
```

profile of v0, /device:TPU:0, one launch (start us, length us, event | category | flops | bytes accessed | tf_op | source)
XLA Modules:
  0.0 524.3 jit_solution(6376675607895804721)
XLA Ops:
  7.2 0.0 reduce-scatter.4.cloned.1.call-start
  7.2 1.3 multiply_reduce_fusion.5
  8.5 42.2 %psum.63 = f32[]{:T(128)} all-reduce(f32[]{:T(128)} %multiply_reduce_fusion.5), channel_id=1, replica_groups=mesh['ray'=4,'vox'=8] {'ray','vox'}, use_global_device_ids=true, to_apply=%region_1.0 | all-reduce | flops 1 | bytes 8 | tf_op jit(solution)/shard_map/psum | solution.py:30
  51.4 0.7 compare_select_fusion
  52.7 0.9 fusion.19
  53.7 0.0 copy-start
  53.7 0.0 copy-start.1
  53.7 5.3 %fusion.26 = f32[64,1,128]{2,1,0:T(1,128)S(1)} fusion(f32[64,128,1]{1,2,0:T(1,128)S(1)} %bitcast.43, f32[64,128,128]{2,1,0:T(8,128)} %param.5), kind=kOutput, calls=%fused_computation.52 | convolution fusion | flops 12582912 | bytes 4259840 | tf_op jit(solution)/shard_map/tij,ti->tj/dot_general | solution.py:24
  59.0 1.5 scatter_custom_fusion
  60.5 0.0 reduce-scatter.4.cloned.1.call-update
  60.5 0.0 reduce-scatter.6.cloned.1.call-start
  60.6 61.7 %reduce-scatter.4.cloned.1.call-done = f32[64,128]{1,0:T(8,128)} async-done(((f32[512,128]{1,0:T(8,128)}), f32[64,128]{1,0:T(8,128)}) %reduce-scatter.4.cloned.1.call-update) | async-done | bytes 32784 | tf_op jit(solution)/shard_map/reduce_scatter | solution.py:26
  122.3 10.8 %psum.64 = f32[64,128]{1,0:T(8,128)S(1)} all-reduce(f32[64,128]{1,0:T(8,128)} %reduce-scatter.4.cloned.1.call-done), channel_id=1, replica_groups=mesh['ray'=4,'vox'=8] {'ray'}, use_global_device_ids=true, to_apply=%region_4.0 | all-reduce | flops 8192 | bytes 65536 | tf_op jit(solution)/shard_map/psum | solution.py:27
  133.1 0.6 multiply_reduce_fusion.2
  133.7 20.1 %psum.65 = f32[]{:T(128)} all-reduce(f32[]{:T(128)} %multiply_reduce_fusion.2), channel_id=1, replica_groups=mesh['ray'=4,'vox'=8] {'vox'}, use_global_device_ids=true, to_apply=%region_6.0 | all-reduce | flops 1 | bytes 8 | tf_op jit(solution)/shard_map/psum | solution.py:33
  154.5 30.9 %all_gather.6 = f32[512,128]{1,0:T(8,128)S(1)} all-gather(f32[64,128]{1,0:T(8,128)S(1)} %broadcast_divide_fusion.1), channel_id=1, replica_groups=mesh['ray'=4,'vox'=8] {'vox'}, dimensions={0}, use_global_device_ids=true | all-gather | bytes 294912 | tf_op jit(solution)/shard_map/all_gather | solution.py:45
  185.4 0.6 gather_fusion
  186.0 8.3 %fusion.27 = f32[64,1,128]{2,1,0:T(1,128)S(1)} fusion(f32[64,128,1]{1,2,0:T(1,128)S(1)} %bitcast.40, f32[64,128,128]{2,1,0:T(8,128)} %param.5), kind=kOutput, calls=%fused_computation.53 | convolution fusion | flops 12582912 | bytes 4259840 | tf_op jit(solution)/shard_map/tij,tj->ti/dot_general | solution.py:46
  194.3 0.0 copy-done
  194.3 0.0 copy-done.1
  194.3 0.8 multiply_reduce_fusion.4
  195.2 37.1 %psum.66 = f32[]{:T(128)} all-reduce(f32[]{:T(128)} %get-tuple-element.4), channel_id=1, replica_groups=mesh['ray'=4,'vox'=8] {'ray','vox'}, use_global_device_ids=true, to_apply=%region_8.0 | all-reduce | flops 1 | bytes 8 | tf_op jit(solution)/shard_map/psum | solution.py:30
  233.0 0.2 fusion.18
  233.2 5.3 %fusion.28 = f32[64,1,128]{2,1,0:T(1,128)S(1)} fusion(f32[64,128,1]{1,2,0:T(1,128)S(1)} %bitcast.44, f32[64,128,128]{2,1,0:T(8,128)} %param.5), kind=kOutput, calls=%fused_computation.54 | convolution fusion | flops 12582912 | bytes 4259840 | tf_op jit(solution)/shard_map/tij,ti->tj/dot_general | solution.py:24
  238.5 1.5 scatter_custom_fusion.1
  240.0 0.0 reduce-scatter.6.cloned.1.call-update
  240.0 0.0 reduce-scatter.8.cloned.1.call-start
  240.1 63.4 %reduce-scatter.6.cloned.1.call-done = f32[64,128]{1,0:T(8,128)} async-done(((f32[512,128]{1,0:T(8,128)}), f32[64,128]{1,0:T(8,128)}) %reduce-scatter.6.cloned.1.call-update) | async-done | bytes 32784 | tf_op jit(solution)/shard_map/reduce_scatter | solution.py:26
  303.4 10.8 %psum.67 = f32[64,128]{1,0:T(8,128)S(1)} all-reduce(f32[64,128]{1,0:T(8,128)} %reduce-scatter.6.cloned.1.call-done), channel_id=1, replica_groups=mesh['ray'=4,'vox'=8] {'ray'}, use_global_device_ids=true, to_apply=%region_11.0 | all-reduce | flops 8192 | bytes 65536 | tf_op jit(solution)/shard_map/psum | solution.py:27
  314.2 0.6 multiply_reduce_fusion.1
  314.9 20.1 %psum.68 = f32[]{:T(128)} all-reduce(f32[]{:T(128)} %multiply_reduce_fusion.1), channel_id=1, replica_groups=mesh['ray'=4,'vox'=8] {'vox'}, use_global_device_ids=true, to_apply=%region_13.0 | all-reduce | flops 1 | bytes 8 | tf_op jit(solution)/shard_map/psum | solution.py:33
  335.7 31.1 %all_gather.7 = f32[512,128]{1,0:T(8,128)S(1)} all-gather(f32[64,128]{1,0:T(8,128)S(1)} %broadcast_divide_fusion), channel_id=1, replica_groups=mesh['ray'=4,'vox'=8] {'vox'}, dimensions={0}, use_global_device_ids=true | all-gather | bytes 294912 | tf_op jit(solution)/shard_map/all_gather | solution.py:45
  366.7 0.6 gather_fusion.1
  367.3 8.3 %fusion.29 = f32[64,1,128]{2,1,0:T(1,128)S(1)} fusion(f32[64,128,1]{1,2,0:T(1,128)S(1)} %bitcast.38, f32[64,128,128]{2,1,0:T(8,128)} %param.5), kind=kOutput, calls=%fused_computation.55 | convolution fusion | flops 12582912 | bytes 4259840 | tf_op jit(solution)/shard_map/tij,tj->ti/dot_general | solution.py:46
  375.6 0.8 multiply_reduce_fusion.3
  376.4 37.1 %psum.69 = f32[]{:T(128)} all-reduce(f32[]{:T(128)} %get-tuple-element.6), channel_id=1, replica_groups=mesh['ray'=4,'vox'=8] {'ray','vox'}, use_global_device_ids=true, to_apply=%region_15.0 | all-reduce | flops 1 | bytes 8 | tf_op jit(solution)/shard_map/psum | solution.py:30
  414.3 0.2 fusion.16
  414.5 5.3 %fusion.30 = f32[64,1,128]{2,1,0:T(1,128)S(1)} fusion(f32[64,128,1]{1,2,0:T(1,128)S(1)} %bitcast.42, f32[64,128,128]{2,1,0:T(8,128)} %param.5), kind=kOutput, calls=%fused_computation.56 | convolution fusion | flops 12582912 | bytes 4259840 | tf_op jit(solution)/shard_map/tij,ti->tj/dot_general | solution.py:24
  419.8 1.5 scatter_custom_fusion.2
  421.3 0.0 reduce-scatter.8.cloned.1.call-update
  421.7 63.1 %reduce-scatter.8.cloned.1.call-done = f32[64,128]{1,0:T(8,128)} async-done(((f32[512,128]{1,0:T(8,128)}), f32[64,128]{1,0:T(8,128)}) %reduce-scatter.8.cloned.1.call-update) | async-done | bytes 32784 | tf_op jit(solution)/shard_map/reduce_scatter | solution.py:26
  484.8 10.8 %psum.70 = f32[64,128]{1,0:T(8,128)S(1)} all-reduce(f32[64,128]{1,0:T(8,128)} %reduce-scatter.8.cloned.1.call-done), channel_id=1, replica_groups=mesh['ray'=4,'vox'=8] {'ray'}, use_global_device_ids=true, to_apply=%region_18.0 | all-reduce | flops 8192 | bytes 65536 | tf_op jit(solution)/shard_map/psum | solution.py:27
  495.6 0.6 multiply_reduce_fusion
  496.2 20.1 %psum.71 = f32[]{:T(128)} all-reduce(f32[]{:T(128)} %multiply_reduce_fusion), channel_id=1, replica_groups=mesh['ray'=4,'vox'=8] {'vox'}, use_global_device_ids=true, to_apply=%region_20.0 | all-reduce | flops 1 | bytes 8 | tf_op jit(solution)/shard_map/psum | solution.py:33
  517.1 0.7 multiply_subtract_fusion
  (4 shorter events, 0.0 us)
Async XLA Ops:
  7.2 115.2 %reduce-scatter.4.cloned.1.call-start = ((), (), s32[]{:S(2)}) async-start(), calls=%async_computation.3 | async-start | bytes 294912 | tf_op jit(solution)/shard_map/reduce_scatter | solution.py:26
  53.7 140.7 %copy-start = (f32[16,128]{1,0:T(8,128)S(1)}, f32[16,128]{1,0:T(8,128)}, u32[]{:S(2)}) copy-start(f32[16,128]{1,0:T(8,128)} %param.9) | copy-start | bytes 24580
  53.7 140.7 %copy-start.1 = (s32[64]{0:T(128)S(1)}, s32[64]{0:T(128)}, u32[]{:S(2)}) copy-start(s32[64]{0:T(128)} %param.6) | copy-start | bytes 772
  60.5 242.9 %reduce-scatter.6.cloned.1.call-start = ((), (), s32[]{:S(2)}) async-start(), calls=%async_computation.4 | async-start | bytes 294912 | tf_op jit(solution)/shard_map/reduce_scatter | solution.py:26
  240.0 244.7 %reduce-scatter.8.cloned.1.call-start = ((), (), s32[]{:S(2)}) async-start(), calls=%async_computation.5 | async-start | bytes 294912 | tf_op jit(solution)/shard_map/reduce_scatter | solution.py:26
Sparse Core Ops, SparseCore 0:
  60.7 61.6 reduce-scatter.3
  240.2 63.2 reduce-scatter.5
  421.5 63.2 reduce-scatter.7
where the time goes:
time: 526 us; the launch traced here: 524 us
  blocking collectives  271 us (52%)
  waiting for transfers between devices  188 us (36%)
  matrix products  35.5 us (7%)
  between operations  19.1 us (4%)
  other arithmetic  9.11 us (2%)
    reduce_scatter x3, waiting for transfers between devices, backward(): lax.psum_scatter(partial_sum, 'vox', scatter_dimension=0, tiled=True)  188 us
    psum x3, blocking collectives, ray_length(): return jnp.sqrt(lax.psum(jnp.sum(ray_vec * ray_vec), ('ray', 'vox')))  116 us
    all_gather x2, blocking collectives, on_device(): whole = lax.all_gather(vox_vec, 'vox', axis=0, tiled=True)  62 us
    psum x3, blocking collectives, vox_length(): return jnp.sqrt(lax.psum(jnp.sum(vox_vec * vox_vec), 'vox'))  60.2 us
    psum x3, blocking collectives, backward(): return lax.psum(owned, 'ray')  32.4 us
    dot_general x2, matrix products, on_device(): jnp.einsum('tij,tj->ti', tiles, whole[tile_vox], precision=HIGH) * live  16.6 us
    dot_general x3, matrix products, backward(): prod = jnp.einsum('tij,ti->tj', tiles, rows_in, precision=HIGH) * live  15.8 us
  transfers between devices with their start and end apart: 3, of which 3 were waited for; matrix products, arithmetic and copies ran while one was open for 0% of the time, Pallas kernels for 0%

commit v1 on v0

--- a/solution.py
+++ b/solution.py
@@ -42,7 +42,15 @@
     phibar = beta_now
     rhobar = alpha_now
     for step in range(ITERS):
-        whole = lax.all_gather(vox_vec, "vox", axis=0, tiled=True)
+        ways, here, lap = (lax.axis_size("vox"), lax.axis_index("vox"), vox_vec.shape[0])
+        line, have = (vox_vec, 1)
+        while have < ways:
+            line = jnp.concatenate(
+                [line, lax.ppermute(line, "vox", [(d, (d - have) % ways) for d in range(ways)])],
+                axis=0,
+            )
+            have = 2 * have
+        whole = jnp.roll(line, here * lap, axis=0)
         forward_prod = jnp.einsum("tij,tj->ti", tiles, whole[tile_vox], precision=HIGH) * live
         ray_vec = jnp.dot(selector, forward_prod, precision=HIGH) - alpha_now * ray_vec
         beta_now = ray_length(ray_vec)

time: 526 us -> 498 us (0.947)
  blocking collectives: 271 us -> 213 us
  waiting for transfers between devices: 188 us -> 217 us
    all_gather x2 -> x0, blocking collectives: 62 us -> none  [on_device(): whole = lax.all_gather(vox_vec, 'vox', axis=0, tiled=True)]
    ppermute x0 -> x6, waiting for transfers between devices: none -> 31 us  [on_device(): lax.ppermute(line, 'vox', [(d, (d - have) % ways) for d in range(ways)])]
  transfers between devices with their start and end apart: 3 -> 9, of which waited for: 3 -> 9; matrix products, arithmetic and copies ran while one was open for 0% -> 0% of each run, Pallas kernels for 0% -> 0%
where the time goes in v1:
time: 498 us; the launch traced here: 496 us
  waiting for transfers between devices  217 us (44%)
  blocking collectives  213 us (43%)
  matrix products  35.5 us (7%)
  between operations  19.2 us (4%)
  other arithmetic  10.3 us (2%)
    reduce_scatter x3, waiting for transfers between devices, backward(): lax.psum_scatter(partial_sum, 'vox', scatter_dimension=0, tiled=True)  186 us
    psum x3, blocking collectives, ray_length(): return jnp.sqrt(lax.psum(jnp.sum(ray_vec * ray_vec), ('ray', 'vox')))  120 us
    psum x3, blocking collectives, vox_length(): return jnp.sqrt(lax.psum(jnp.sum(vox_vec * vox_vec), 'vox'))  60.3 us
    psum x3, blocking collectives, backward(): return lax.psum(owned, 'ray')  32.4 us
    ppermute x6, waiting for transfers between devices, on_device(): lax.ppermute(line, 'vox', [(d, (d - have) % ways) for d in range(ways)])  31 us
    dot_general x2, matrix products, on_device(): jnp.einsum('tij,tj->ti', tiles, whole[tile_vox], precision=HIGH) * live  16.6 us
    dot_general x3, matrix products, backward(): prod = jnp.einsum('tij,ti->tj', tiles, rows_in, precision=HIGH) * live  15.8 us
  transfers between devices with their start and end apart: 9, of which 9 were waited for; matrix products, arithmetic and copies ran while one was open for 0% of the time, Pallas kernels for 0%

profile of v1, /device:TPU:0, one launch (start us, length us, event | category | flops | bytes accessed | tf_op | source)
XLA Modules:
  0.0 496.3 jit_solution(4568662209399585600)
XLA Ops:
  7.2 0.0 reduce-scatter.4.cloned.1.call-start
  7.2 1.3 multiply_reduce_fusion.5
  8.5 42.2 %psum.63 = f32[]{:T(128)} all-reduce(f32[]{:T(128)} %multiply_reduce_fusion.5), channel_id=1, replica_groups=mesh['ray'=4,'vox'=8] {'ray','vox'}, use_global_device_ids=true, to_apply=%region_1.0 | all-reduce | flops 1 | bytes 8 | tf_op jit(solution)/shard_map/psum | solution.py:30
  51.4 0.7 compare_select_fusion
  52.7 0.9 fusion.33
  53.7 5.3 %fusion.40 = f32[64,1,128]{2,1,0:T(1,128)S(1)} fusion(f32[64,128,1]{1,2,0:T(1,128)S(1)} %bitcast.43, f32[64,128,128]{2,1,0:T(8,128)} %param.7), kind=kOutput, calls=%fused_computation.86 | convolution fusion | flops 12582912 | bytes 4259840 | tf_op jit(solution)/shard_map/tij,ti->tj/dot_general | solution.py:24
  59.0 1.5 scatter_custom_fusion
  60.5 0.0 reduce-scatter.6.cloned.1.call-start
  60.6 61.7 %reduce-scatter.4.cloned.1.call-done = f32[64,128]{1,0:T(8,128)} async-done(((f32[512,128]{1,0:T(8,128)}), f32[64,128]{1,0:T(8,128)}) %reduce-scatter.4.cloned.1.call-update) | async-done | bytes 32784 | tf_op jit(solution)/shard_map/reduce_scatter | solution.py:26
  122.3 10.8 %psum.64 = f32[64,128]{1,0:T(8,128)S(1)} all-reduce(f32[64,128]{1,0:T(8,128)} %reduce-scatter.4.cloned.1.call-done), channel_id=1, replica_groups=mesh['ray'=4,'vox'=8] {'ray'}, use_global_device_ids=true, to_apply=%region_4.0 | all-reduce | flops 8192 | bytes 65536 | tf_op jit(solution)/shard_map/psum | solution.py:27
  133.1 0.6 multiply_reduce_fusion.2
  133.7 20.1 %psum.65 = f32[]{:T(128)} all-reduce(f32[]{:T(128)} %multiply_reduce_fusion.2), channel_id=1, replica_groups=mesh['ray'=4,'vox'=8] {'vox'}, use_global_device_ids=true, to_apply=%region_6.0 | all-reduce | flops 1 | bytes 8 | tf_op jit(solution)/shard_map/psum | solution.py:33
  154.5 0.1 collective-permute-start
  154.6 3.9 collective-permute-done
  158.5 5.4 %collective-permute-done.1 = f32[128,128]{1,0:T(8,128)S(1)} collective-permute-done((f32[128,128]{1,0:T(8,128)S(1)}, f32[128,128]{1,0:T(8,128)S(1)}, u32[]{:S(2)}, u32[]{:S(2)}) %collective-permute-start.1) | collective-permute-done | bytes 65568 | tf_op jit(solution)/shard_map/ppermute | solution.py:49
  163.9 0.1 collective-permute-start.2
  164.0 6.2 %collective-permute-done.2 = f32[256,128]{1,0:T(8,128)S(1)} collective-permute-done((f32[256,128]{1,0:T(8,128)S(1)}, f32[256,128]{1,0:T(8,128)S(1)}, u32[]{:S(2)}, u32[]{:S(2)}) %collective-permute-start.2) | collective-permute-done | bytes 131104 | tf_op jit(solution)/shard_map/ppermute | solution.py:49
  170.2 0.6 fusion.10
  170.8 0.6 gather_fusion
  171.4 8.3 %fusion.41 = f32[64,1,128]{2,1,0:T(1,128)S(1)} fusion(f32[64,128,1]{1,2,0:T(1,128)S(1)} %bitcast.40, f32[64,128,128]{2,1,0:T(8,128)} %param.7), kind=kOutput, calls=%fused_computation.87 | convolution fusion | flops 12582912 | bytes 4259840 | tf_op jit(solution)/shard_map/tij,tj->ti/dot_general | solution.py:54
  179.7 0.8 multiply_reduce_fusion.4
  180.5 39.0 %psum.66 = f32[]{:T(128)} all-reduce(f32[]{:T(128)} %get-tuple-element.5), channel_id=1, replica_groups=mesh['ray'=4,'vox'=8] {'ray','vox'}, use_global_device_ids=true, to_apply=%region_8.10 | all-reduce | flops 1 | bytes 8 | tf_op jit(solution)/shard_map/psum | solution.py:30
  220.2 0.2 fusion.32
  220.4 5.3 %fusion.42 = f32[64,1,128]{2,1,0:T(1,128)S(1)} fusion(f32[64,128,1]{1,2,0:T(1,128)S(1)} %bitcast.44, f32[64,128,128]{2,1,0:T(8,128)} %param.7), kind=kOutput, calls=%fused_computation.88 | convolution fusion | flops 12582912 | bytes 4259840 | tf_op jit(solution)/shard_map/tij,ti->tj/dot_general | solution.py:24
  225.7 1.5 scatter_custom_fusion.1
  227.3 0.0 reduce-scatter.8.cloned.1.call-start
  227.3 62.3 %reduce-scatter.6.cloned.1.call-done = f32[64,128]{1,0:T(8,128)} async-done(((f32[512,128]{1,0:T(8,128)}), f32[64,128]{1,0:T(8,128)}) %reduce-scatter.6.cloned.1.call-update) | async-done | bytes 32784 | tf_op jit(solution)/shard_map/reduce_scatter | solution.py:26
  289.6 10.8 %psum.67 = f32[64,128]{1,0:T(8,128)S(1)} all-reduce(f32[64,128]{1,0:T(8,128)} %reduce-scatter.6.cloned.1.call-done), channel_id=1, replica_groups=mesh['ray'=4,'vox'=8] {'ray'}, use_global_device_ids=true, to_apply=%region_11.13 | all-reduce | flops 8192 | bytes 65536 | tf_op jit(solution)/shard_map/psum | solution.py:27
  300.4 0.6 multiply_reduce_fusion.1
  301.0 20.1 %psum.68 = f32[]{:T(128)} all-reduce(f32[]{:T(128)} %multiply_reduce_fusion.1), channel_id=1, replica_groups=mesh['ray'=4,'vox'=8] {'vox'}, use_global_device_ids=true, to_apply=%region_13.15 | all-reduce | flops 1 | bytes 8 | tf_op jit(solution)/shard_map/psum | solution.py:33
  321.8 0.1 collective-permute-start.3
  321.9 3.9 collective-permute-done.3
  325.8 5.3 %collective-permute-done.4 = f32[128,128]{1,0:T(8,128)S(1)} collective-permute-done((f32[128,128]{1,0:T(8,128)S(1)}, f32[128,128]{1,0:T(8,128)S(1)}, u32[]{:S(2)}, u32[]{:S(2)}) %collective-permute-start.4) | collective-permute-done | bytes 65568 | tf_op jit(solution)/shard_map/ppermute | solution.py:49
  331.2 0.1 collective-permute-start.5
  331.2 6.3 %collective-permute-done.5 = f32[256,128]{1,0:T(8,128)S(1)} collective-permute-done((f32[256,128]{1,0:T(8,128)S(1)}, f32[256,128]{1,0:T(8,128)S(1)}, u32[]{:S(2)}, u32[]{:S(2)}) %collective-permute-start.5) | collective-permute-done | bytes 131104 | tf_op jit(solution)/shard_map/ppermute | solution.py:49
  337.5 0.6 fusion.3
  338.1 0.6 gather_fusion.1
  338.7 8.3 %fusion.43 = f32[64,1,128]{2,1,0:T(1,128)S(1)} fusion(f32[64,128,1]{1,2,0:T(1,128)S(1)} %bitcast.38, f32[64,128,128]{2,1,0:T(8,128)} %param.7), kind=kOutput, calls=%fused_computation.89 | convolution fusion | flops 12582912 | bytes 4259840 | tf_op jit(solution)/shard_map/tij,tj->ti/dot_general | solution.py:54
  347.0 0.8 multiply_reduce_fusion.3
  347.8 39.0 %psum.69 = f32[]{:T(128)} all-reduce(f32[]{:T(128)} %get-tuple-element.7), channel_id=1, replica_groups=mesh['ray'=4,'vox'=8] {'ray','vox'}, use_global_device_ids=true, to_apply=%region_15.17 | all-reduce | flops 1 | bytes 8 | tf_op jit(solution)/shard_map/psum | solution.py:30
  387.5 0.2 fusion.30
  387.7 5.3 %fusion.44 = f32[64,1,128]{2,1,0:T(1,128)S(1)} fusion(f32[64,128,1]{1,2,0:T(1,128)S(1)} %bitcast.42, f32[64,128,128]{2,1,0:T(8,128)} %param.7), kind=kOutput, calls=%fused_computation.90 | convolution fusion | flops 12582912 | bytes 4259840 | tf_op jit(solution)/shard_map/tij,ti->tj/dot_general | solution.py:24
  393.0 1.5 scatter_custom_fusion.2
  394.9 61.9 %reduce-scatter.8.cloned.1.call-done = f32[64,128]{1,0:T(8,128)} async-done(((f32[512,128]{1,0:T(8,128)}), f32[64,128]{1,0:T(8,128)}) %reduce-scatter.8.cloned.1.call-update) | async-done | bytes 32784 | tf_op jit(solution)/shard_map/reduce_scatter | solution.py:26
  456.8 10.8 %psum.70 = f32[64,128]{1,0:T(8,128)S(1)} all-reduce(f32[64,128]{1,0:T(8,128)} %reduce-scatter.8.cloned.1.call-done), channel_id=1, replica_groups=mesh['ray'=4,'vox'=8] {'ray'}, use_global_device_ids=true, to_apply=%region_18.20 | all-reduce | flops 8192 | bytes 65536 | tf_op jit(solution)/shard_map/psum | solution.py:27
  467.6 0.6 multiply_reduce_fusion
  468.3 20.1 %psum.71 = f32[]{:T(128)} all-reduce(f32[]{:T(128)} %multiply_reduce_fusion), channel_id=1, replica_groups=mesh['ray'=4,'vox'=8] {'vox'}, use_global_device_ids=true, to_apply=%region_20.22 | all-reduce | flops 1 | bytes 8 | tf_op jit(solution)/shard_map/psum | solution.py:33
  489.2 0.7 multiply_subtract_fusion
  (17 shorter events, 0.1 us)
Async XLA Ops:
  7.2 115.2 %reduce-scatter.4.cloned.1.call-start = ((), (), s32[]{:S(2)}) async-start(), calls=%async_computation.3 | async-start | bytes 294912 | tf_op jit(solution)/shard_map/reduce_scatter | solution.py:26
  53.7 126.0 %copy-start = (f32[16,128]{1,0:T(8,128)S(1)}, f32[16,128]{1,0:T(8,128)}, u32[]{:S(2)}) copy-start(f32[16,128]{1,0:T(8,128)} %param.11) | copy-start | bytes 24580
  53.7 126.0 %copy-start.1 = (s32[64]{0:T(128)S(1)}, s32[64]{0:T(128)}, u32[]{:S(2)}) copy-start(s32[64]{0:T(128)} %param.8) | copy-start | bytes 772
  60.5 229.0 %reduce-scatter.6.cloned.1.call-start = ((), (), s32[]{:S(2)}) async-start(), calls=%async_computation.4 | async-start | bytes 294912 | tf_op jit(solution)/shard_map/reduce_scatter | solution.py:26
  154.5 4.0 collective-permute-start
  158.5 5.4 %collective-permute-start.1 = (f32[128,128]{1,0:T(8,128)S(1)}, f32[128,128]{1,0:T(8,128)S(1)}, u32[]{:S(2)}, u32[]{:S(2)}) collective-permute-start(f32[128,128]{1,0:T(8,128)S(1)} %pad_maximum_fusion.2), channel_id=1, source_target_pairs={{0,6},{1,7},{2,0},{3,1},{4,2},{5,3},{6,4},{7,5},{8,14},{9,15},{10,... | collective-permute-start | bytes 196616 | tf_op jit(solution)/shard_map/ppermute | solution.py:49
  163.9 6.3 %collective-permute-start.2 = (f32[256,128]{1,0:T(8,128)S(1)}, f32[256,128]{1,0:T(8,128)S(1)}, u32[]{:S(2)}, u32[]{:S(2)}) collective-permute-start(f32[256,128]{1,0:T(8,128)S(1)} %pad_maximum_fusion), channel_id=1, source_target_pairs={{0,4},{1,5},{2,6},{3,7},{4,0},{5,1},{6,2},{7,3},{8,12},{9,13},{10,... | collective-permute-start | bytes 393224 | tf_op jit(solution)/shard_map/ppermute | solution.py:49
  227.3 229.6 %reduce-scatter.8.cloned.1.call-start = ((), (), s32[]{:S(2)}) async-start(), calls=%async_computation.5 | async-start | bytes 294912 | tf_op jit(solution)/shard_map/reduce_scatter | solution.py:26
  321.8 4.0 collective-permute-start.3
  325.8 5.3 %collective-permute-start.4 = (f32[128,128]{1,0:T(8,128)S(1)}, f32[128,128]{1,0:T(8,128)S(1)}, u32[]{:S(2)}, u32[]{:S(2)}) collective-permute-start(f32[128,128]{1,0:T(8,128)S(1)} %pad_maximum_fusion.3), channel_id=1, source_target_pairs={{0,6},{1,7},{2,0},{3,1},{4,2},{5,3},{6,4},{7,5},{8,14},{9,15},{10,... | collective-permute-start | bytes 196616 | tf_op jit(solution)/shard_map/ppermute | solution.py:49
  331.2 6.3 %collective-permute-start.5 = (f32[256,128]{1,0:T(8,128)S(1)}, f32[256,128]{1,0:T(8,128)S(1)}, u32[]{:S(2)}, u32[]{:S(2)}) collective-permute-start(f32[256,128]{1,0:T(8,128)S(1)} %pad_maximum_fusion.1), channel_id=1, source_target_pairs={{0,4},{1,5},{2,6},{3,7},{4,0},{5,1},{6,2},{7,3},{8,12},{9,13},{10,... | collective-permute-start | bytes 393224 | tf_op jit(solution)/shard_map/ppermute | solution.py:49
Sparse Core Ops, SparseCore 0:
  60.7 61.6 reduce-scatter.3
  227.4 62.1 reduce-scatter.5
  394.7 62.1 reduce-scatter.7
